TPU v7x, 32 devices: a whole 2x2x4 slice. The times are simulated.
32 devices in a mesh: gx: 4 (over y, x), gy: 4 (over z), gz: 2 (over core).
Axes of the slice: x: 2, y: 2, z: 4, core: 2. Of those that a mesh axis runs over, the one named last changes fastest.
Arguments:
- rhs: float32 [7, 7, 7, 4, 16, 256], P(None, None, None, 'gx', 'gy', 'gz'), may hold values from -6 to 6
- orders: int32 [4, 16, 256], P('gx', 'gy', 'gz'), may hold values from 3 to 6
Outputs:
- smoothed: float32 [7, 7, 7, 4, 16, 256], P(None, None, None, 'gx', 'gy', 'gz')
- coarse_residual: float32 [4, 16, 256], P('gx', 'gy')
All inputs are finite; a program needn't handle non-finite values.
Results may differ from a plain program's by a relative error of at most 0.00016.
Values sent between devices are 32-bit elements; how exact they have to be, the bound alone decides.
A program may use at most 64 MiB of HBM per device.

v0:
```python
import functools

import jax
import jax.numpy as jnp
import numpy as np
from jax import lax
from jax.experimental import pallas as pl
from jax.experimental.pallas import tpu as pltpu
from jax.sharding import PartitionSpec as P

PENALTY = 49.0
EIGEN_HIGH = 2.4
EIGEN_LOW = 0.24
MODES = 7
MESH = pl.DeviceIdType.MESH


def tables():
    degree = np.arange(MODES)
    normed = np.sqrt((2.0 * degree + 1.0) / 2.0)
    smaller = np.minimum(degree[:, None], degree[None, :])
    parity = (degree[:, None] + degree[None, :]) % 2 == 0
    stiffness = np.where(parity, normed[:, None] * normed[None, :] * smaller * (smaller + 1), 0.0)
    signs = (-1.0) ** degree
    slope = normed * degree * (degree + 1) / 2.0
    low, low_slope = normed * signs, -slope * signs
    own = stiffness + np.outer(normed, PENALTY * normed - 0.5 * slope) - 0.5 * np.outer(slope, normed)
    own = own + np.outer(low, PENALTY * low + 0.5 * low_slope) + 0.5 * np.outer(low_slope, low)
    one_axis = normed * normed * degree * (degree + 1) + 2.0 * (
        PENALTY * normed * normed - normed * slope
    )
    diagonal = (
        one_axis[:, None, None] + one_axis[None, :, None] + one_axis[None, None, :]
    ) / PENALTY
    return (
        own / PENALTY,
        0.5 * slope - PENALTY * normed,
        0.5 * normed,
        normed / PENALTY,
        slope / PENALTY,
        diagonal,
    )


OWN, JUMP, HALF, VALUE, SLOPE, DIAGONAL = tables()
THETA = 0.5 * (EIGEN_HIGH + EIGEN_LOW)
DELTA = 0.5 * (EIGEN_HIGH - EIGEN_LOW)
RHO_FIRST = DELTA / THETA
RHO_SECOND = 1.0 / (2.0 * THETA / DELTA - RHO_FIRST)
KEEP = 1.0 + RHO_SECOND * RHO_FIRST
STEP = 2.0 * RHO_SECOND / DELTA * THETA


def combine(weights, values):
    total = None
    for weight, value in zip(weights, values):
        term = value * float(weight)
        total = term if total is None else total + term
    return total


def traces(values):
    even, odd = values[0::2], values[1::2]
    jump_even, jump_odd = combine(JUMP[0::2], even), combine(JUMP[1::2], odd)
    half_even, half_odd = combine(HALF[0::2], even), combine(HALF[1::2], odd)
    down = (jump_even - jump_odd, half_even - half_odd)
    up = (jump_even + jump_odd, half_even + half_odd)
    return down, up


def own_row(row, values):
    start = row % 2
    return combine(OWN[row, start::2], values[start::2])


def face_terms(from_up, from_down):
    both = (from_up[0] + from_down[0], from_up[1] + from_down[1])
    apart = (from_up[0] - from_down[0], from_up[1] - from_down[1])

    def term(mode):
        pair = both if mode % 2 == 0 else apart
        if mode == 0:
            return pair[0] * float(VALUE[0])
        return pair[0] * float(VALUE[mode]) + pair[1] * float(SLOPE[mode])

    return term


def vertex_pair(zero, one):
    flat, tilt = np.sqrt(0.5) * zero, (np.sqrt(1.5) / 3.0) * one
    return flat - tilt, flat + tilt


def kernel(
    sizes, cells_y, cells_z, rhs_hbm, orders_ref, table_ref, out_hbm, coarse_ref,
    rhs, first, acc, smooth,
    xs, xr, ys, yr, zs, zr, y_up, y_down,
    xs2, xr2, ys2, yr2, zs2, zr2, y_up2, y_down2, acc2, shift_buf,
    main, top, main_in, top_in,
    local_sem, send_sem, recv_sem,
):
    nx, ny, nz = sizes
    x, y, z = lax.axis_index("gx"), lax.axis_index("gy"), lax.axis_index("gz")
    barrier = pltpu.get_barrier_semaphore()

    def neighbour(axis, sign):
        here = (x, y, z)[axis]
        to = [x, y, z]
        to[axis] = here + sign
        back = [x, y, z]
        back[axis] = here - sign
        below, above = here > 0, here < sizes[axis] - 1
        return (tuple(to), below if sign < 0 else above, tuple(back), above if sign < 0 else below)

    halos = [neighbour(axis, sign) for axis in range(3) for sign in (-1, 1)]
    always = x >= 0
    carries = []
    for i in range(2):
        for j in range(2):
            for r in range(nz):
                if i == 0 and j == 0 and r == 0:
                    continue
                to = (x + i, y + j, lax.rem(z + r, nz))
                source = lax.rem(z - r + nz, nz)
                back = (x - i, y - j, source)
                ok_to, ok_from = always, always
                if i:
                    ok_to, ok_from = ok_to & (x < nx - 1), ok_from & (x > 0)
                if j:
                    ok_to, ok_from = ok_to & (y < ny - 1), ok_from & (y > 0)
                carries.append((to, ok_to, back, ok_from, i, j, source))

    expected = jnp.int32(0)
    for entry in halos + carries:
        to, ok_to, back, ok_from = entry[:4]

        @pl.when(ok_from)
        def _(back=back):
            pl.semaphore_signal(barrier, inc=1, device_id=back, device_id_type=MESH)

        expected = expected + jnp.where(ok_to, 1, 0).astype(jnp.int32)

    load = pltpu.make_async_copy(rhs_hbm, rhs, local_sem.at[0])
    load.start()

    def remote(src, dst, slot, to):
        return pltpu.make_async_remote_copy(
            src_ref=src, dst_ref=dst, send_sem=send_sem.at[slot], recv_sem=recv_sem.at[slot],
            device_id=to, device_id_type=MESH,
        )

    def start(index, slot, src, dst):
        to, ok_to = halos[index][:2]

        @pl.when(ok_to)
        def _():
            remote(src, dst, slot, to).start()

    def receive(index, slot, src, dst):
        to, _, _, ok_from = halos[index]

        @pl.when(ok_from)
        def _():
            remote(src, dst, slot, to).wait_recv()

    def finish(index, slot, src, dst):
        to, ok_to = halos[index][:2]

        @pl.when(ok_to)
        def _():
            remote(src, dst, slot, to).wait_send()

    stages = (((xs, xr), (ys, yr), (zs, zr)), ((xs2, xr2), (ys2, yr2), (zs2, zr2)))

    def over(action, stage, axis):
        src, dst = stages[stage][axis]
        for side in range(2):
            index = 2 * axis + side
            action(index, 6 * stage + index, src.at[side], dst.at[side])

    for stage in range(2):
        for axis in range(3):
            for side in range(2):
                dst = stages[stage][axis][1]

                @pl.when(jnp.logical_not(halos[2 * axis + side][3]))
                def _(dst=dst, side=side):
                    dst[side] = jnp.zeros(dst.shape[1:], jnp.float32)

    orders = orders_ref[0]
    tile = (MODES, cells_y, cells_z)
    last_mode = lax.broadcasted_iota(jnp.int32, tile, 0)
    lane = lax.broadcasted_iota(jnp.int32, (1, 1, cells_z), 2)
    load.wait()

    def active(a, b):
        return jnp.maximum(jnp.maximum(a, b), last_mode) <= orders[None]

    def loop(body):
        def step(index, carry):
            body(index)
            return carry

        lax.fori_loop(0, MODES, step, 0)

    def x_traces(b):
        values = []
        for a in range(MODES):
            value = jnp.where(active(a, b), table_ref[a, b] * rhs[a, b], 0.0)
            first[a, b] = value
            values.append(value)
        sides = traces(values)
        for side in range(2):
            for kind in range(2):
                xs[side, kind, b] = sides[side][kind]

    loop(x_traces)
    pl.semaphore_wait(barrier, expected)
    over(start, 0, 0)

    def y_faces(a, values, send, up_buf, down_buf):
        down, up = traces(values)
        for kind in range(2):
            up_buf[kind, a, :, 0:cells_y, :] = down[kind]
            down_buf[kind, a, :, 1 : cells_y + 1, :] = up[kind]
            send[0, kind, a] = down[kind][:, 0:1, :]
            send[1, kind, a] = up[kind][:, cells_y - 1 : cells_y, :]

    def y_neighbours(a, received, up_buf, down_buf):
        for kind in range(2):
            up_buf[kind, a, :, cells_y : cells_y + 1, :] = received[0, kind, a]
            down_buf[kind, a, :, 0:1, :] = received[1, kind, a]
        return face_terms(
            [up_buf[kind, a, :, 1 : cells_y + 1, :] for kind in range(2)],
            [down_buf[kind, a, :, 0:cells_y, :] for kind in range(2)],
        )

    def z_faces(a, values, send):
        sides = traces(values)
        for side in range(2):
            for kind in range(2):
                send[side, kind, a] = sides[side][kind]

    def z_neighbours(a, send, received):
        def moved(side, kind, edge, amount):
            picked = jnp.where(lane == edge, received[side, kind, a], send[side, kind, a])
            return pltpu.roll(picked, amount, 2)

        return face_terms(
            [moved(0, kind, 0, cells_z - 1) for kind in range(2)],
            [moved(1, kind, cells_z - 1, 1) for kind in range(2)],
        )

    loop(lambda a: z_faces(a, [first[a, :, e] for e in range(MODES)], zs))
    over(start, 0, 2)
    loop(lambda a: y_faces(a, [first[a, b] for b in range(MODES)], ys, y_up, y_down))
    over(start, 0, 1)

    def x_own(b):
        values = [first[a, b] for a in range(MODES)]
        for a in range(MODES):
            acc[a, b] = own_row(a, values)

    def y_own(a):
        values = [first[a, b] for b in range(MODES)]
        for b in range(MODES):
            acc[a, b] += own_row(b, values)

    def z_own(a):
        values = [first[a, :, e] for e in range(MODES)]
        for e in range(MODES):
            acc[a, :, e] += own_row(e, values)

    loop(x_own)
    loop(y_own)
    loop(z_own)

    over(receive, 0, 2)

    def z_flux(a):
        term = z_neighbours(a, zs, zr)
        for e in range(MODES):
            acc[a, :, e] += term(e)

    loop(z_flux)
    over(receive, 0, 1)

    def y_flux(a):
        term = y_neighbours(a, yr, y_up, y_down)
        for b in range(MODES):
            acc[a, b] += term(b)

    loop(y_flux)
    over(receive, 0, 0)

    def x_flux(b):
        term = face_terms(
            [xr[0, kind, b] for kind in range(2)], [xr[1, kind, b] for kind in range(2)]
        )
        for a in range(MODES):
            right = rhs[a, b]
            total = acc[a, b] + term(a)
            value = table_ref[a, b] * (KEEP * right + STEP * (right - total))
            smooth[a, b] = jnp.where(active(a, b), value, 0.0)

    loop(x_flux)
    store = pltpu.make_async_copy(smooth, out_hbm, local_sem.at[1])
    store.start()

    for b in range(2):
        values = [smooth[a, b, 0:2] for a in range(MODES)]
        sides = traces(values)
        for side in range(2):
            for kind in range(2):
                xs2[side, kind, b] = sides[side][kind]
    over(start, 1, 0)
    for a in range(2):
        y_faces(a, [smooth[a, b, 0:2] for b in range(MODES)], ys2, y_up2, y_down2)
    over(start, 1, 1)
    for a in range(2):
        z_faces(a, [smooth[a, 0:2, e] for e in range(MODES)], zs2)
    over(start, 1, 2)
    for b in range(2):
        values = [smooth[a, b, 0:2] for a in range(MODES)]
        for a in range(2):
            acc2[a, b] = own_row(a, values)
    for a in range(2):
        values = [smooth[a, b, 0:2] for b in range(MODES)]
        for b in range(2):
            acc2[a, b] += own_row(b, values)
        values = [smooth[a, 0:2, e] for e in range(MODES)]
        for e in range(2):
            acc2[a, :, e] += own_row(e, values)
    over(receive, 1, 2)
    for a in range(2):
        term = z_neighbours(a, zs2, zr2)
        for e in range(2):
            acc2[a, :, e] += term(e)
    over(receive, 1, 1)
    for a in range(2):
        term = y_neighbours(a, yr2, y_up2, y_down2)
        for b in range(2):
            acc2[a, b] += term(b)
    over(receive, 1, 0)
    for b in range(2):
        term = face_terms(
            [xr2[0, kind, b] for kind in range(2)], [xr2[1, kind, b] for kind in range(2)]
        )
        for a in range(2):
            acc2[a, b] += term(a)

    resid = {}
    for a in range(2):
        for b in range(2):
            for e in range(2):
                left = rhs[a, b, e] - acc2[a, b, e]
                resid[a, b, e] = jnp.where(orders >= max(a, b, e), left, 0.0)
    for axis in range(3):
        done = {}
        for key in resid:
            if key[axis] == 0:
                other = tuple(1 if n == axis else key[n] for n in range(3))
                done[key], done[other] = vertex_pair(resid[key], resid[other])
        resid = done

    for i in range(2):
        for k in range(2):
            shift_buf[i, k, 0:1, :] = jnp.zeros((1, cells_z), jnp.float32)
            shift_buf[i, k, 1 : cells_y + 1, :] = resid[i, 1, k]
            main[i, k] = resid[i, 0, k] + shift_buf[i, k, 0:cells_y, :]
            top[i, k] = resid[i, 1, k][cells_y - 1 : cells_y, :]

    @pl.when(x == 0)
    def _():
        main_in[1] = jnp.zeros(main_in.shape[1:], jnp.float32)
        top_in[1] = jnp.zeros(top_in.shape[1:], jnp.float32)

    @pl.when(y == 0)
    def _():
        top_in[...] = jnp.zeros(top_in.shape, jnp.float32)

    def carry(number):
        to, ok_to, _, ok_from, i, j, source = carries[number]
        src, dst = (top, top_in) if j else (main, main_in)
        return (
            ok_to, ok_from, remote(src.at[i], dst.at[i, z], 12 + number, to),
            remote(src.at[i], dst.at[i, source], 12 + number, to),
        )

    for number in range(len(carries)):
        ok_to = carries[number][1]

        @pl.when(ok_to)
        def _(number=number):
            carry(number)[2].start()

    main_in[0, pl.ds(z, 1)] = main[0][None]

    for number in range(len(carries)):
        ok_from = carries[number][3]

        @pl.when(ok_from)
        def _(number=number):
            carry(number)[3].wait_recv()

    row = lax.broadcasted_iota(jnp.int32, (cells_y, cells_z), 0)
    column = lax.broadcasted_iota(jnp.int32, (cells_y, cells_z), 1)
    below = jnp.zeros((cells_y, cells_z), jnp.float32)
    for zz in range(nz):
        sums = []
        for k in range(2):
            total = main_in[0, zz, k] + main_in[1, zz, k]
            extra = top_in[0, zz, k] + top_in[1, zz, k]
            sums.append(total + jnp.where(row == 0, extra, 0.0))
        moved = pltpu.roll(jnp.where(column == cells_z - 1, below, sums[1]), 1, 1)
        below = sums[1]
        inside = (x > 0) & ((row > 0) | (y > 0))
        if zz == 0:
            inside = inside & (column > 0)
        coarse_ref[0, :, zz * cells_z : (zz + 1) * cells_z] = jnp.where(
            inside, sums[0] + moved, 0.0
        )

    for stage in range(2):
        for axis in range(3):
            over(finish, stage, axis)
    for number in range(len(carries)):
        ok_to = carries[number][1]

        @pl.when(ok_to)
        def _(number=number):
            carry(number)[2].wait_send()

    store.wait()


def per_device(sizes, rhs, orders):
    _, cells_y, cells_z = orders.shape
    nz = sizes[2]
    table = jnp.asarray(
        np.broadcast_to(
            (1.0 / (DIAGONAL * THETA))[:, :, :, None, None], DIAGONAL.shape + (1, cells_z)
        ),
        jnp.float32,
    )
    field = rhs.reshape(rhs.shape[:3] + rhs.shape[4:])
    cells = (cells_y, cells_z)
    rows = 8 * ((cells_y + 8) // 8)

    def buf(*shape):
        return pltpu.VMEM(shape, jnp.float32)

    def halo(n):
        line = (2, 2, n, n)
        return [
            buf(*line, *cells), buf(*line, *cells),
            buf(*line, 1, cells_z), buf(*line, 1, cells_z),
            buf(*line, *cells), buf(*line, *cells),
            buf(2, n, n, rows, cells_z), buf(2, n, n, rows, cells_z),
        ]

    slots = 12 + 4 * nz - 1
    vmem = pl.BlockSpec(memory_space=pltpu.VMEM)
    hbm = pl.BlockSpec(memory_space=pl.ANY)
    smoothed, coarse = pl.pallas_call(
        functools.partial(kernel, sizes, cells_y, cells_z),
        out_shape=(
            jax.ShapeDtypeStruct(field.shape, jnp.float32),
            jax.ShapeDtypeStruct((1, cells_y, nz * cells_z), jnp.float32),
        ),
        in_specs=[hbm, vmem, vmem],
        out_specs=(hbm, vmem),
        scratch_shapes=[buf(*field.shape)] * 4
        + halo(MODES)
        + halo(2)
        + [
            buf(2, 2, 2, *cells), buf(2, 2, rows, cells_z),
            buf(2, 2, *cells), buf(2, 2, 1, cells_z),
            buf(2, nz, 2, *cells), buf(2, nz, 2, 1, cells_z),
            pltpu.SemaphoreType.DMA((2,)),
            pltpu.SemaphoreType.DMA((slots,)),
            pltpu.SemaphoreType.DMA((slots,)),
        ],
        compiler_params=pltpu.CompilerParams(collective_id=0, has_side_effects=True),
        name="smoother",
    )(field, orders, table)
    return smoothed.reshape(rhs.shape), coarse


def solution(mesh):
    sizes = tuple(mesh.shape[axis] for axis in ("gx", "gy", "gz"))
    return jax.shard_map(
        functools.partial(per_device, sizes),
        mesh=mesh,
        in_specs=(P(None, None, None, "gx", "gy", "gz"), P("gx", "gy", "gz")),
        out_specs=(P(None, None, None, "gx", "gy", "gz"), P("gx", "gy", None)),
        check_vma=False,
    )
```

profile of v0, /device:TPU:13, one launch (start us, length us, event | category | flops | bytes accessed | tf_op | source)
XLA Modules:
  0.0 26.4 jit_solution(7877143320941358568)
XLA Ops:
  0.6 23.1 %smoother.1 = (f32[7,7,7,4,128]{4,3,2,1,0:T(4,128)}, f32[1,4,256]{2,1,0:T(4,128)}) custom-call(f32[7,7,7,4,128]{4,3,2,1,0:T(4,128)} %bitcast.4, s32[1,4,128]{2,1,0:T(4,128)} %orders_ref.1, f32[7,7,7,1,128]{4,3,2,1,0:T(1,128)} %constant.2.clone.table_ref), custom_call_target="tpu_custom_call" | custom-call | tf_op jit(solution)/shard_map/smoother/pallas_call | solution.py:465
  23.8 0.0 copy-start
  23.8 2.0 %copy.8 = f32[7,7,7,1,4,128]{5,4,3,2,1,0:T(4,128)} copy(f32[7,7,7,1,4,128]{5,4,3,2,1,0:T(4,128)} %bitcast.5) | data formatting | bytes 1404928
  25.8 0.0 copy-done
  25.8 0.6 %copy.9 = f32[1,4,256]{2,1,0:T(4,128)} copy(f32[1,4,256]{2,1,0:T(4,128)S(1)} %copy-done) | data formatting | bytes 8192
Async XLA Ops:
  23.8 2.0 %copy-start = (f32[1,4,256]{2,1,0:T(4,128)S(1)}, f32[1,4,256]{2,1,0:T(4,128)}, u32[]{:S(2)}) copy-start(f32[1,4,256]{2,1,0:T(4,128)} %get-tuple-element.11) | copy-start | bytes 12292
where the time goes:
time: 26.6 us; the launch traced here: 26.4 us
  Pallas kernels  23.1 us (87%)
  local copies, waits for them, and re-layouts  2.61 us (10%)
  between operations  0.65 us (2%)
    pallas_call x1, Pallas kernels, per_device(): pl.pallas_call(functools.partial(kernel, sizes, cells_y, cells_z), out_sh...  23.1 us
    unnamed x4, local copies, waits for them, and re-layouts  2.61 us

commit v1 on v0

--- a/solution.py
+++ b/solution.py
@@ -12,6 +12,7 @@
 EIGEN_HIGH = 2.4
 EIGEN_LOW = 0.24
 MODES = 7
+RELAYED = 3
 MESH = pl.DeviceIdType.MESH
 
 
@@ -92,12 +93,12 @@
 
 
 def kernel(
-    sizes, cells_y, cells_z, rhs_hbm, orders_ref, table_ref, out_hbm, coarse_ref,
-    rhs, first, acc, smooth,
+    sizes, cells_y, cells_z, rhs_hbm, orders_hbm, table_hbm, smooth, coarse_ref,
+    rhs, first, acc, orders_ref, table_ref,
     xs, xr, ys, yr, zs, zr, y_up, y_down,
     xs2, xr2, ys2, yr2, zs2, zr2, y_up2, y_down2, acc2, shift_buf,
     main, top, main_in, top_in,
-    local_sem, send_sem, recv_sem,
+    relay, local_sem, send_sem, recv_sem, x_send, x_recv, relay_in, relay_out,
 ):
     nx, ny, nz = sizes
     x, y, z = lax.axis_index("gx"), lax.axis_index("gy"), lax.axis_index("gz")
@@ -130,8 +131,15 @@
                     ok_to, ok_from = ok_to & (y < ny - 1), ok_from & (y > 0)
                 carries.append((to, ok_to, back, ok_from, i, j, source))
 
+    odd = lax.rem(x, 2) == 1
+    even = jnp.logical_not(odd)
+    relays = (
+        ((x - 2, y, z), even & (x >= 2), (x + 2, y, z), even & (x + 2 < nx), (x + 1, y, z)),
+        ((x + 2, y, z), odd & (x + 2 < nx), (x - 2, y, z), odd & (x >= 3), (x - 1, y, z)),
+    )
+
     expected = jnp.int32(0)
-    for entry in halos + carries:
+    for entry in halos + list(relays) + carries:
         to, ok_to, back, ok_from = entry[:4]
 
         @pl.when(ok_from)
@@ -140,8 +148,18 @@
 
         expected = expected + jnp.where(ok_to, 1, 0).astype(jnp.int32)
 
-    load = pltpu.make_async_copy(rhs_hbm, rhs, local_sem.at[0])
-    load.start()
+    loads = [
+        pltpu.make_async_copy(orders_hbm, orders_ref, local_sem.at[MODES]),
+        pltpu.make_async_copy(table_hbm, table_ref, local_sem.at[MODES + 1]),
+    ]
+    for copy in loads:
+        copy.start()
+
+    def rhs_load(b):
+        return pltpu.make_async_copy(rhs_hbm.at[:, b], rhs.at[:, b], local_sem.at[b])
+
+    for b in range(MODES):
+        rhs_load(b).start()
 
     def remote(src, dst, slot, to):
         return pltpu.make_async_remote_copy(
@@ -187,11 +205,12 @@
                 def _(dst=dst, side=side):
                     dst[side] = jnp.zeros(dst.shape[1:], jnp.float32)
 
+    for copy in loads:
+        copy.wait()
     orders = orders_ref[0]
     tile = (MODES, cells_y, cells_z)
     last_mode = lax.broadcasted_iota(jnp.int32, tile, 0)
     lane = lax.broadcasted_iota(jnp.int32, (1, 1, cells_z), 2)
-    load.wait()
 
     def active(a, b):
         return jnp.maximum(jnp.maximum(a, b), last_mode) <= orders[None]
@@ -203,7 +222,75 @@
 
         lax.fori_loop(0, MODES, step, 0)
 
+    def x_copy(side, b, to):
+        return pltpu.make_async_remote_copy(
+            src_ref=xs.at[side, b], dst_ref=xr.at[side, b],
+            send_sem=x_send.at[side, b], recv_sem=x_recv.at[side, b],
+            device_id=to, device_id_type=MESH,
+        )
+
+    def to_relay(side, b, to):
+        return pltpu.make_async_remote_copy(
+            src_ref=xs.at[side, b], dst_ref=relay.at[side, b],
+            send_sem=x_send.at[side, b], recv_sem=relay_in.at[side, b],
+            device_id=to, device_id_type=MESH,
+        )
+
+    def from_relay(side, b, to):
+        return pltpu.make_async_remote_copy(
+            src_ref=relay.at[side, b], dst_ref=xr.at[side, b],
+            send_sem=relay_out.at[side, b], recv_sem=x_recv.at[side, b],
+            device_id=to, device_id_type=MESH,
+        )
+
+    def x_start(b):
+        for side in range(2):
+            to, ok_to = halos[side][:2]
+            via, used = relays[side][:2]
+            detour = used & (b < RELAYED)
+
+            @pl.when(detour)
+            def _():
+                to_relay(side, b, via).start()
+
+            @pl.when(ok_to & jnp.logical_not(detour))
+            def _():
+                x_copy(side, b, to).start()
+
+    def forward(b):
+        for side in range(2):
+            back, relaying, target = relays[side][2:]
+
+            @pl.when(relaying)
+            def _():
+                to_relay(side, b, target).wait_recv()
+                from_relay(side, b, target).start()
+
+    def x_receive(b):
+        for side in range(2):
+
+            @pl.when(halos[side][3])
+            def _():
+                x_copy(side, b, halos[side][0]).wait_recv()
+
+    def x_finish(b):
+        for side in range(2):
+
+            @pl.when(halos[side][1])
+            def _():
+                x_copy(side, b, halos[side][0]).wait_send()
+
+    def relay_finish(b):
+        for side in range(2):
+
+            @pl.when(relays[side][3])
+            def _():
+                from_relay(side, b, relays[side][4]).wait_send()
+
+    pl.semaphore_wait(barrier, expected)
+
     def x_traces(b):
+        rhs_load(b).wait()
         values = []
         for a in range(MODES):
             value = jnp.where(active(a, b), table_ref[a, b] * rhs[a, b], 0.0)
@@ -212,11 +299,10 @@
         sides = traces(values)
         for side in range(2):
             for kind in range(2):
-                xs[side, kind, b] = sides[side][kind]
+                xs[side, b, kind] = sides[side][kind]
+        x_start(b)
 
     loop(x_traces)
-    pl.semaphore_wait(barrier, expected)
-    over(start, 0, 0)
 
     def y_faces(a, values, send, up_buf, down_buf):
         down, up = traces(values)
@@ -272,8 +358,11 @@
             acc[a, :, e] += own_row(e, values)
 
     loop(x_own)
+    forward(0)
     loop(y_own)
+    forward(1)
     loop(z_own)
+    forward(2)
 
     over(receive, 0, 2)
 
@@ -291,11 +380,12 @@
             acc[a, b] += term(b)
 
     loop(y_flux)
-    over(receive, 0, 0)
-
-    def x_flux(b):
+
+    def x_flux(index):
+        b = lax.rem(index + RELAYED, MODES)
+        x_receive(b)
         term = face_terms(
-            [xr[0, kind, b] for kind in range(2)], [xr[1, kind, b] for kind in range(2)]
+            [xr[0, b, kind] for kind in range(2)], [xr[1, b, kind] for kind in range(2)]
         )
         for a in range(MODES):
             right = rhs[a, b]
@@ -304,8 +394,6 @@
             smooth[a, b] = jnp.where(active(a, b), value, 0.0)
 
     loop(x_flux)
-    store = pltpu.make_async_copy(smooth, out_hbm, local_sem.at[1])
-    store.start()
 
     for b in range(2):
         values = [smooth[a, b, 0:2] for a in range(MODES)]
@@ -379,20 +467,17 @@
     def _():
         top_in[...] = jnp.zeros(top_in.shape, jnp.float32)
 
-    def carry(number):
-        to, ok_to, _, ok_from, i, j, source = carries[number]
+    def carry(number, arriving):
+        to, _, _, _, i, j, source = carries[number]
         src, dst = (top, top_in) if j else (main, main_in)
-        return (
-            ok_to, ok_from, remote(src.at[i], dst.at[i, z], 12 + number, to),
-            remote(src.at[i], dst.at[i, source], 12 + number, to),
-        )
+        return remote(src.at[i], dst.at[i, source if arriving else z], 12 + number, to)
 
     for number in range(len(carries)):
         ok_to = carries[number][1]
 
         @pl.when(ok_to)
         def _(number=number):
-            carry(number)[2].start()
+            carry(number, False).start()
 
     main_in[0, pl.ds(z, 1)] = main[0][None]
 
@@ -401,7 +486,7 @@
 
         @pl.when(ok_from)
         def _(number=number):
-            carry(number)[3].wait_recv()
+            carry(number, True).wait_recv()
 
     row = lax.broadcasted_iota(jnp.int32, (cells_y, cells_z), 0)
     column = lax.broadcasted_iota(jnp.int32, (cells_y, cells_z), 1)
@@ -423,15 +508,17 @@
 
     for stage in range(2):
         for axis in range(3):
-            over(finish, stage, axis)
+            if (stage, axis) != (0, 0):
+                over(finish, stage, axis)
+    loop(x_finish)
+    for b in range(RELAYED):
+        relay_finish(b)
     for number in range(len(carries)):
         ok_to = carries[number][1]
 
         @pl.when(ok_to)
         def _(number=number):
-            carry(number)[2].wait_send()
-
-    store.wait()
+            carry(number, False).wait_send()
 
 
 def per_device(sizes, rhs, orders):
@@ -452,8 +539,9 @@
 
     def halo(n):
         line = (2, 2, n, n)
+        x_line = (2, n, 2, n) if n == MODES else line
         return [
-            buf(*line, *cells), buf(*line, *cells),
+            buf(*x_line, *cells), buf(*x_line, *cells),
             buf(*line, 1, cells_z), buf(*line, 1, cells_z),
             buf(*line, *cells), buf(*line, *cells),
             buf(2, n, n, rows, cells_z), buf(2, n, n, rows, cells_z),
@@ -461,27 +549,33 @@
 
     slots = 12 + 4 * nz - 1
     vmem = pl.BlockSpec(memory_space=pltpu.VMEM)
-    hbm = pl.BlockSpec(memory_space=pl.ANY)
+    hbm = pl.BlockSpec(memory_space=pltpu.HBM)
     smoothed, coarse = pl.pallas_call(
         functools.partial(kernel, sizes, cells_y, cells_z),
         out_shape=(
-            jax.ShapeDtypeStruct(field.shape, jnp.float32),
-            jax.ShapeDtypeStruct((1, cells_y, nz * cells_z), jnp.float32),
+            pltpu.VMEM(field.shape, jnp.float32),
+            pltpu.VMEM((1, cells_y, nz * cells_z), jnp.float32),
         ),
-        in_specs=[hbm, vmem, vmem],
-        out_specs=(hbm, vmem),
-        scratch_shapes=[buf(*field.shape)] * 4
+        in_specs=[hbm, hbm, hbm],
+        out_specs=(vmem, vmem),
+        scratch_shapes=[buf(*field.shape)] * 3
+        + [pltpu.VMEM(orders.shape, jnp.int32), buf(*table.shape)]
         + halo(MODES)
         + halo(2)
         + [
             buf(2, 2, 2, *cells), buf(2, 2, rows, cells_z),
             buf(2, 2, *cells), buf(2, 2, 1, cells_z),
             buf(2, nz, 2, *cells), buf(2, nz, 2, 1, cells_z),
-            pltpu.SemaphoreType.DMA((2,)),
+            buf(2, RELAYED, 2, MODES, *cells),
+            pltpu.SemaphoreType.DMA((MODES + 2,)),
             pltpu.SemaphoreType.DMA((slots,)),
             pltpu.SemaphoreType.DMA((slots,)),
+            pltpu.SemaphoreType.DMA((2, MODES)),
+            pltpu.SemaphoreType.DMA((2, MODES)),
+            pltpu.SemaphoreType.DMA((2, RELAYED)),
+            pltpu.SemaphoreType.DMA((2, RELAYED)),
         ],
-        compiler_params=pltpu.CompilerParams(collective_id=0, has_side_effects=True),
+        compiler_params=pltpu.CompilerParams(collective_id=0, has_side_effects=True, vmem_limit_bytes=24 * 2**20),
         name="smoother",
     )(field, orders, table)
     return smoothed.reshape(rhs.shape), coarse

time: 26.6 us -> 24.7 us (0.929)
  Pallas kernels: 23.1 us -> 19.7 us
  local copies, waits for them, and re-layouts: 2.61 us -> 4.14 us
    pallas_call x1, Pallas kernels: 23.1 us -> 19.7 us  [per_device(): pl.pallas_call(functools.partial(kernel, sizes, cells_y, cells_z), out_sh...]
    unnamed x4 -> x8, local copies, waits for them, and re-layouts: 2.61 us -> 4.14 us
where the time goes in v1:
time: 24.7 us; the launch traced here: 24.5 us
  Pallas kernels  19.7 us (80%)
  local copies, waits for them, and re-layouts  4.14 us (17%)
  between operations  0.65 us (3%)
    pallas_call x1, Pallas kernels, per_device(): pl.pallas_call(functools.partial(kernel, sizes, cells_y, cells_z), out_sh...  19.7 us
    unnamed x8, local copies, waits for them, and re-layouts  4.14 us

profile of v1, /device:TPU:13, one launch (start us, length us, event | category | flops | bytes accessed | tf_op | source)
XLA Modules:
  0.0 24.5 jit_solution(2440737543000048346)
XLA Ops:
  0.6 0.0 copy-start
  0.6 1.1 %copy-done = f32[7,7,7,1,4,128]{5,4,3,2,1,0:T(4,128)S(1)} copy-done((f32[7,7,7,1,4,128]{5,4,3,2,1,0:T(4,128)S(1)}, f32[7,7,7,1,4,128]{5,4,3,2,1,0:T(4,128)}, u32[]{:S(2)}) %copy-start) | copy-done | bytes 702488
  1.7 0.0 copy-start.1
  1.7 0.9 %copy-done.1 = f32[7,7,7,1,128]{4,3,2,1,0:T(1,128)S(1)} copy-done((f32[7,7,7,1,128]{4,3,2,1,0:T(1,128)S(1)}, f32[7,7,7,1,128]{4,3,2,1,0:T(1,128)}, u32[]{:S(2)}) %copy-start.1) | copy-done | bytes 175640
  2.7 0.0 copy-start.2
  2.7 0.7 %copy-done.2 = s32[1,4,128]{2,1,0:T(4,128)S(1)} copy-done((s32[1,4,128]{2,1,0:T(4,128)S(1)}, s32[1,4,128]{2,1,0:T(4,128)}, u32[]{:S(2)}) %copy-start.2) | copy-done | bytes 2072
  3.3 19.7 %smoother.1 = (f32[7,7,7,4,128]{4,3,2,1,0:T(4,128)S(1)}, f32[1,4,256]{2,1,0:T(4,128)S(1)}) custom-call(f32[7,7,7,4,128]{4,3,2,1,0:T(4,128)S(1)} %bitcast.5, s32[1,4,128]{2,1,0:T(4,128)S(1)} %copy-done.2, f32[7,7,7,1,128]{4,3,2,1,0:T(1,128)S(1)} %copy-done.1), custom_call_target="tpu_custom_call" | custom-call | tf_op jit(solution)/shard_map/smoother/pallas_call | solution.py:553
  23.0 0.9 %copy.8 = f32[7,7,7,1,4,128]{5,4,3,2,1,0:T(4,128)} copy(f32[7,7,7,1,4,128]{5,4,3,2,1,0:T(4,128)S(1)} %bitcast.4) | data formatting | bytes 1404928
  23.9 0.6 %copy.9 = f32[1,4,256]{2,1,0:T(4,128)} copy(f32[1,4,256]{2,1,0:T(4,128)S(1)} %get-tuple-element.9) | data formatting | bytes 8192
Async XLA Ops:
  0.6 1.1 %copy-start = (f32[7,7,7,1,4,128]{5,4,3,2,1,0:T(4,128)S(1)}, f32[7,7,7,1,4,128]{5,4,3,2,1,0:T(4,128)}, u32[]{:S(2)}) copy-start(f32[7,7,7,1,4,128]{5,4,3,2,1,0:T(4,128)} %param.3) | copy-start | bytes 2107396
  1.7 0.9 %copy-start.1 = (f32[7,7,7,1,128]{4,3,2,1,0:T(1,128)S(1)}, f32[7,7,7,1,128]{4,3,2,1,0:T(1,128)}, u32[]{:S(2)}) copy-start(f32[7,7,7,1,128]{4,3,2,1,0:T(1,128)} %constant.2.clone.table_hbm) | copy-start | bytes 526852
  2.7 0.7 %copy-start.2 = (s32[1,4,128]{2,1,0:T(4,128)S(1)}, s32[1,4,128]{2,1,0:T(4,128)}, u32[]{:S(2)}) copy-start(s32[1,4,128]{2,1,0:T(4,128)} %orders_hbm.1) | copy-start | bytes 6148

commit v2 on v1

--- a/solution.py
+++ b/solution.py
@@ -139,7 +139,7 @@
     )
 
     expected = jnp.int32(0)
-    for entry in halos + list(relays) + carries:
+    for entry in halos + list(relays):
         to, ok_to, back, ok_from = entry[:4]
 
         @pl.when(ok_from)
@@ -575,7 +575,7 @@
             pltpu.SemaphoreType.DMA((2, RELAYED)),
             pltpu.SemaphoreType.DMA((2, RELAYED)),
         ],
-        compiler_params=pltpu.CompilerParams(collective_id=0, has_side_effects=True, vmem_limit_bytes=24 * 2**20),
+        compiler_params=pltpu.CompilerParams(collective_id=0, has_side_effects=True),
         name="smoother",
     )(field, orders, table)
     return smoothed.reshape(rhs.shape), coarse

time: 24.7 us -> 20.5 us (0.83)
  local copies, waits for them, and re-layouts: 4.14 us -> 1.45 us
  Pallas kernels: 19.7 us -> 18.3 us
    unnamed x8 -> x2, local copies, waits for them, and re-layouts: 4.14 us -> 1.45 us
    pallas_call x1, Pallas kernels: 19.7 us -> 18.3 us  [per_device(): pl.pallas_call(functools.partial(kernel, sizes, cells_y, cells_z), out_sh...]
where the time goes in v2:
time: 20.5 us; the launch traced here: 20.4 us
  Pallas kernels  18.3 us (89%)
  local copies, waits for them, and re-layouts  1.45 us (7%)
  between operations  0.64 us (3%)
    pallas_call x1, Pallas kernels, per_device(): pl.pallas_call(functools.partial(kernel, sizes, cells_y, cells_z), out_sh...  18.3 us
    unnamed x2, local copies, waits for them, and re-layouts  1.45 us

profile of v2, /device:TPU:13, one launch (start us, length us, event | category | flops | bytes accessed | tf_op | source)
XLA Modules:
  0.0 20.4 jit_solution(7190475306048822222)
XLA Ops:
  0.6 18.3 %smoother.1 = (f32[7,7,7,4,128]{4,3,2,1,0:T(4,128)S(1)}, f32[1,4,256]{2,1,0:T(4,128)S(1)}) custom-call(f32[7,7,7,4,128]{4,3,2,1,0:T(4,128)} %bitcast.5, s32[1,4,128]{2,1,0:T(4,128)} %orders_hbm.1, f32[7,7,7,1,128]{4,3,2,1,0:T(1,128)} %constant.2.clone.table_hbm), custom_call_target="tpu_custom_call" | custom-call | tf_op jit(solution)/shard_map/smoother/pallas_call | solution.py:553
  18.9 0.9 %copy.8 = f32[7,7,7,1,4,128]{5,4,3,2,1,0:T(4,128)} copy(f32[7,7,7,1,4,128]{5,4,3,2,1,0:T(4,128)S(1)} %bitcast.4) | data formatting | bytes 1404928
  19.8 0.6 %copy.9 = f32[1,4,256]{2,1,0:T(4,128)} copy(f32[1,4,256]{2,1,0:T(4,128)S(1)} %get-tuple-element.9) | data formatting | bytes 8192
